TPU v7x, 256 devices: a whole 4x4x8 slice. The times are simulated.
256 devices in a mesh: gx: 8 (over y, core), gy: 4 (over z_lo), gz: 8 (over z_hi, x).
Axes of the slice: x: 4, y: 4, z: 8 (z_hi: 2, z_lo: 4; z = z_hi * 4 + z_lo), core: 2. Of those that a mesh axis runs over, the one named last changes fastest.
Arguments:
- tokens: bfloat16 [2048, 8192], P(('gx', 'gy'), 'gz'), may hold values from -6 to 6
- gate_weight: bfloat16 [8192, 28672], P('gz', ('gx', 'gy')), may hold values from -0.0625 to 0.0625
- up_weight: bfloat16 [8192, 28672], P('gz', ('gx', 'gy')), may hold values from -0.0625 to 0.0625
- down_weight: bfloat16 [28672, 8192], P(('gx', 'gy'), 'gz'), may hold values from -0.03125 to 0.03125
Outputs:
- layer_output: bfloat16 [2048, 8192], P(('gx', 'gy'), 'gz')
All inputs are finite; a program needn't handle non-finite values.
Results may differ from a plain program's by a relative error of at most 0.029.
Values may be sent and summed in bfloat16 or wider, within the bound.
A program may use at most 128 MiB of HBM per device.

v0:
```python
import jax
import jax.numpy as jnp
from jax import lax
from jax.sharding import PartitionSpec as P


def shards(tokens, gate_weight, up_weight, down_weight):
    gathered = lax.all_gather(tokens, "gx", axis=0, tiled=True)

    def column_product(weight_piece):
        return jnp.dot(gathered, weight_piece, preferred_element_type=jnp.float32)

    gate_partial = column_product(lax.all_gather(gate_weight, "gy", axis=1, tiled=True))
    up_partial = column_product(lax.all_gather(up_weight, "gy", axis=1, tiled=True))
    gate_sum, up_sum = (
        lax.psum_scatter(
            gate_partial.astype(jnp.bfloat16), "gz", scatter_dimension=0, tiled=True
        ).astype(jnp.float32),
        lax.psum_scatter(
            up_partial.astype(jnp.bfloat16), "gz", scatter_dimension=0, tiled=True
        ).astype(jnp.float32),
    )
    local_hidden = (jax.nn.silu(gate_sum) * up_sum).astype(jnp.bfloat16)
    hidden = lax.all_gather(local_hidden, "gz", axis=0, tiled=True)
    down_partial = jnp.dot(
        hidden,
        lax.all_gather(down_weight, "gy", axis=0, tiled=True),
        preferred_element_type=jnp.float32,
    )
    layer_output = lax.psum_scatter(
        down_partial.astype(jnp.bfloat16), "gx", scatter_dimension=0, tiled=True
    )
    return layer_output


def solution(mesh):
    return jax.shard_map(
        shards,
        mesh=mesh,
        in_specs=(
            P(("gx", "gy"), "gz"),
            P("gz", ("gx", "gy")),
            P("gz", ("gx", "gy")),
            P(("gx", "gy"), "gz"),
        ),
        out_specs=P(("gx", "gy"), "gz"),
        check_vma=False,
    )
```

profile of v0, /device:TPU:2, one launch (start us, length us, event | category | flops | bytes accessed | tf_op | source)
XLA Modules:
  0.0 839.3 jit_solution(120754620333667691)
XLA Ops:
  6.5 0.0 all-gather.6.cloned.1.call-start
  6.5 0.7 all-gather.6.cloned.1.call-update
  7.3 0.0 all-gather.8.cloned.1.call-start
  7.3 0.7 all-gather.8.cloned.1.call-update
  8.0 0.0 all-gather.10.cloned.1.call-start
  8.1 0.7 all-gather.10.cloned.1.call-update
  8.7 0.0 reduce-scatter.4.cloned.1.call-start
  8.8 29.3 %all-gather.6.cloned.1.call-done = bf16[512,1024]{1,0:T(8,128)(2,1)} async-done(((bf16[64,1024]{1,0:T(8,128)(2,1)}), bf16[512,1024]{1,0:T(8,128)(2,1)}) %all-gather.6.cloned.1.call-update) | async-done | bytes 1048592 | tf_op jit(solution)/shard_map/all_gather | solution.py:8
  38.1 0.0 copy-start
  38.1 137.6 %all-gather.8.cloned.1.call-done = bf16[1024,3584]{1,0:T(8,128)(2,1)} async-done(((bf16[1024,896]{1,0:T(8,128)(2,1)}), bf16[1024,3584]{1,0:T(8,128)(2,1)}) %all-gather.8.cloned.1.call-update) | async-done | bytes 7340048 | tf_op jit(solution)/shard_map/all_gather | solution.py:13
  175.7 9.2 %convolution_convert_fusion.1 = bf16[512,3584]{1,0:T(8,128)(2,1)} fusion(bf16[512,1024]{1,0:T(8,128)(2,1)} %all-gather.6.cloned.1.call-done, bf16[1024,3584]{1,0:T(8,128)(2,1)} %all-gather.8.cloned.1.call-done), kind=kOutput, calls=%fused_computation.1 | convolution fusion | flops 3759931392 | bytes 12058624 | tf_op jit(solution)/shard_map/dot_general | solution.py:11
  184.9 0.0 reduce-scatter.4.cloned.1.call-update
  184.9 0.0 reduce-scatter.6.cloned.1.call-start
  185.0 128.1 %all-gather.10.cloned.1.call-done = bf16[1024,3584]{1,0:T(8,128)(2,1)} async-done(((bf16[1024,896]{1,0:T(8,128)(2,1)}), bf16[1024,3584]{1,0:T(8,128)(2,1)}) %all-gather.10.cloned.1.call-update) | async-done | bytes 7340048 | tf_op jit(solution)/shard_map/all_gather | solution.py:14
  313.1 0.0 copy-done
  313.1 8.4 %convolution_convert_fusion = bf16[512,3584]{1,0:T(8,128)(2,1)} fusion(bf16[512,1024]{1,0:T(8,128)(2,1)S(1)} %copy-done, bf16[1024,3584]{1,0:T(8,128)(2,1)} %all-gather.10.cloned.1.call-done), kind=kOutput, calls=%fused_computation | convolution fusion | flops 3759931392 | bytes 12058624 | tf_op jit(solution)/shard_map/dot_general | solution.py:11
  321.5 0.0 reduce-scatter.6.cloned.1.call-update
  321.6 0.0 all-gather.14.cloned.1.call-start
  321.6 0.5 all-gather.14.cloned.1.call-update
  322.1 0.0 all-gather.12.cloned.1.call-start
  322.2 115.4 %reduce-scatter.4.cloned.1.call-done = bf16[64,3584]{1,0:T(8,128)(2,1)} async-done(((bf16[512,3584]{1,0:T(8,128)(2,1)}), bf16[64,3584]{1,0:T(8,128)(2,1)}) %reduce-scatter.4.cloned.1.call-update) | async-done | bytes 458768 | tf_op jit(solution)/shard_map/reduce_scatter | solution.py:16
  437.6 121.3 %reduce-scatter.6.cloned.1.call-done = bf16[64,3584]{1,0:T(8,128)(2,1)} async-done(((bf16[512,3584]{1,0:T(8,128)(2,1)}), bf16[64,3584]{1,0:T(8,128)(2,1)}) %reduce-scatter.6.cloned.1.call-update) | async-done | bytes 458768 | tf_op jit(solution)/shard_map/reduce_scatter | solution.py:19
  558.9 2.2 fusion.4
  561.1 0.0 all-gather.12.cloned.1.call-update
  561.1 0.0 reduce-scatter.8.cloned.1.call-start
  561.2 131.1 %all-gather.14.cloned.1.call-done = bf16[3584,1024]{1,0:T(8,128)(2,1)} async-done(((bf16[896,1024]{1,0:T(8,128)(2,1)}), bf16[3584,1024]{1,0:T(8,128)(2,1)}) %all-gather.14.cloned.1.call-update) | async-done | bytes 7340048 | tf_op jit(solution)/shard_map/all_gather | solution.py:27
  692.3 100.6 %all-gather.12.cloned.1.call-done = bf16[512,3584]{1,0:T(8,128)(2,1)} async-done(((bf16[64,3584]{1,0:T(8,128)(2,1)}), bf16[512,3584]{1,0:T(8,128)(2,1)}) %all-gather.12.cloned.1.call-update) | async-done | bytes 3670032 | tf_op jit(solution)/shard_map/all_gather | solution.py:24
  792.9 9.1 %convolution_convert_fusion.2 = bf16[512,1024]{1,0:T(8,128)(2,1)} fusion(bf16[512,3584]{1,0:T(8,128)(2,1)} %all-gather.12.cloned.1.call-done, bf16[3584,1024]{1,0:T(8,128)(2,1)} %all-gather.14.cloned.1.call-done), kind=kOutput, calls=%fused_computation.2 | convolution fusion | flops 3758620672 | bytes 12058624 | tf_op jit(solution)/shard_map/dot_general | solution.py:25
  802.0 0.0 reduce-scatter.8.cloned.1.call-update
  802.0 30.5 %reduce-scatter.8.cloned.1.call-done = bf16[64,1024]{1,0:T(8,128)(2,1)} async-done(((bf16[512,1024]{1,0:T(8,128)(2,1)}), bf16[64,1024]{1,0:T(8,128)(2,1)}) %reduce-scatter.8.cloned.1.call-update) | async-done | bytes 131088 | tf_op jit(solution)/shard_map/reduce_scatter | solution.py:30
Async XLA Ops:
  6.5 31.6 %all-gather.6.cloned.1.call-start = ((), (), s32[]{:S(2)}) async-start(), calls=%async_computation.3 | async-start | bytes 1179648 | tf_op jit(solution)/shard_map/all_gather | solution.py:8
  7.3 168.4 %all-gather.8.cloned.1.call-start = ((), (), s32[]{:S(2)}) async-start(), calls=%async_computation.4 | async-start | bytes 9175040 | tf_op jit(solution)/shard_map/all_gather | solution.py:13
  8.0 305.1 %all-gather.10.cloned.1.call-start = ((), (), s32[]{:S(2)}) async-start(), calls=%async_computation.6 | async-start | bytes 9175040 | tf_op jit(solution)/shard_map/all_gather | solution.py:14
  8.7 428.9 %reduce-scatter.4.cloned.1.call-start = ((), (), s32[]{:S(2)}) async-start(), calls=%async_computation.5 | async-start | bytes 4128768 | tf_op jit(solution)/shard_map/reduce_scatter | solution.py:16
  38.1 275.0 %copy-start = (bf16[512,1024]{1,0:T(8,128)(2,1)S(1)}, bf16[512,1024]{1,0:T(8,128)(2,1)}, u32[]{:S(2)}) copy-start(bf16[512,1024]{1,0:T(8,128)(2,1)} %all-gather.6.cloned.1.call-done) | copy-start | bytes 3145732
  184.9 374.0 %reduce-scatter.6.cloned.1.call-start = ((), (), s32[]{:S(2)}) async-start(), calls=%async_computation.7 | async-start | bytes 4128768 | tf_op jit(solution)/shard_map/reduce_scatter | solution.py:19
  321.6 370.7 %all-gather.14.cloned.1.call-start = ((), (), s32[]{:S(2)}) async-start(), calls=%async_computation.9 | async-start | bytes 9175040 | tf_op jit(solution)/shard_map/all_gather | solution.py:27
  322.1 470.7 %all-gather.12.cloned.1.call-start = ((), (), s32[]{:S(2)}) async-start(), calls=%async_computation.8 | async-start | bytes 4128768 | tf_op jit(solution)/shard_map/all_gather | solution.py:24
  561.1 271.4 %reduce-scatter.8.cloned.1.call-start = ((), (), s32[]{:S(2)}) async-start(), calls=%async_computation.10 | async-start | bytes 1179648 | tf_op jit(solution)/shard_map/reduce_scatter | solution.py:30
Sparse Core Ops, SparseCore 0:
  9.2 28.8 all-gather.5
  40.0 135.6 all-gather.7
  177.5 135.5 all-gather.9
  317.2 120.3 reduce-scatter.3
  442.3 116.5 reduce-scatter.5
  560.6 131.6 all-gather.13
  694.9 97.9 all-gather.11
  802.1 30.3 reduce-scatter.7
where the time goes:
time: 839 us
  waiting for transfers between devices  797 us (95%)
  matrix products  26.8 us (3%)
  between operations  13.5 us (2%)
    all_gather x1, waiting for transfers between devices, shards(): lax.all_gather(gate_weight, 'gy', axis=1, tiled=True)  138 us
    all_gather x1, waiting for transfers between devices, shards(): lax.all_gather(down_weight, 'gy', axis=0, tiled=True)  131 us
    all_gather x1, waiting for transfers between devices, shards(): lax.all_gather(up_weight, 'gy', axis=1, tiled=True)  128 us
    reduce_scatter x1, waiting for transfers between devices, shards(): lax.psum_scatter(up_partial.astype(jnp.bfloat16), 'gz', scatter_dimension...  121 us
    reduce_scatter x1, waiting for transfers between devices, shards(): lax.psum_scatter(gate_partial.astype(jnp.bfloat16), 'gz', scatter_dimensi...  115 us
    all_gather x1, waiting for transfers between devices, shards(): hidden = lax.all_gather(local_hidden, 'gz', axis=0, tiled=True)  101 us
    reduce_scatter x1, waiting for transfers between devices, shards(): lax.psum_scatter(down_partial.astype(jnp.bfloat16), 'gx', scatter_dimensi...  30.5 us
    all_gather x1, waiting for transfers between devices, shards(): gathered = lax.all_gather(tokens, 'gx', axis=0, tiled=True)  29.3 us
  transfers between devices with their start and end apart: 8, of which 8 were waited for; matrix products, arithmetic and copies ran while one was open for 2% of the time, Pallas kernels for 0%

commit v1 on v0

--- a/solution.py
+++ b/solution.py
@@ -22,10 +22,21 @@
     )
     local_hidden = (jax.nn.silu(gate_sum) * up_sum).astype(jnp.bfloat16)
     hidden = lax.all_gather(local_hidden, "gz", axis=0, tiled=True)
+
+    def plan_the_scenes(content, axis_tag):
+        z = jnp.concatenate(
+            jax.lax.all_to_all(
+                jnp.stack(jax.lax.axis_size(axis_tag) * [content], axis=0),
+                axis_name=axis_tag,
+                split_axis=0,
+                concat_axis=0,
+            ),
+            0,
+        )
+        return z
+
     down_partial = jnp.dot(
-        hidden,
-        lax.all_gather(down_weight, "gy", axis=0, tiled=True),
-        preferred_element_type=jnp.float32,
+        hidden, plan_the_scenes(down_weight, "gy"), preferred_element_type=jnp.float32
     )
     layer_output = lax.psum_scatter(
         down_partial.astype(jnp.bfloat16), "gx", scatter_dimension=0, tiled=True

time: 839 us -> 787 us (0.938)
  waiting for transfers between devices: 797 us -> 734 us
    all_gather x1 -> x0, waiting for transfers between devices: 131 us -> none  [shards(): lax.all_gather(down_weight, 'gy', axis=0, tiled=True)]
    reduce_scatter x1, waiting for transfers between devices: 115 us -> 164 us  [shards(): lax.psum_scatter(gate_partial.astype(jnp.bfloat16), 'gz', scatter_dimensi...]
    reduce_scatter x1, waiting for transfers between devices: 121 us -> 149 us  [shards(): lax.psum_scatter(up_partial.astype(jnp.bfloat16), 'gz', scatter_dimension...]
  transfers between devices with their start and end apart: 8 -> 8, of which waited for: 8 -> 7; matrix products, arithmetic and copies ran while one was open for 2% -> 3% of each run, Pallas kernels for 0% -> 0%
where the time goes in v1:
time: 787 us
  waiting for transfers between devices  734 us (93%)
  matrix products  26.9 us (3%)
  between operations  13.5 us (2%)
    reduce_scatter x1, waiting for transfers between devices, shards(): lax.psum_scatter(gate_partial.astype(jnp.bfloat16), 'gz', scatter_dimensi...  164 us
    reduce_scatter x1, waiting for transfers between devices, shards(): lax.psum_scatter(up_partial.astype(jnp.bfloat16), 'gz', scatter_dimension...  149 us
    all_gather x1, waiting for transfers between devices, shards(): lax.all_gather(gate_weight, 'gy', axis=1, tiled=True)  138 us
    all_gather x1, waiting for transfers between devices, shards(): lax.all_gather(up_weight, 'gy', axis=1, tiled=True)  128 us
    all_gather x1, waiting for transfers between devices, shards(): hidden = lax.all_gather(local_hidden, 'gz', axis=0, tiled=True)  94.3 us
    reduce_scatter x1, waiting for transfers between devices, shards(): lax.psum_scatter(down_partial.astype(jnp.bfloat16), 'gx', scatter_dimensi...  30.5 us
    all_gather x1, waiting for transfers between devices, shards(): gathered = lax.all_gather(tokens, 'gx', axis=0, tiled=True)  29.3 us
    dot_general x2, matrix products, column_product(): return jnp.dot(gathered, weight_piece, preferred_element_type=jnp.float32)  17.7 us
  transfers between devices with their start and end apart: 8, of which 7 were waited for; matrix products, arithmetic and copies ran while one was open for 3% of the time, Pallas kernels for 0%

profile of v1, /device:TPU:2, one launch (start us, length us, event | category | flops | bytes accessed | tf_op | source)
XLA Modules:
  0.0 786.6 jit_solution(17991095188411551644)
XLA Ops:
  6.5 0.0 all-gather.5.cloned.1.call-start
  6.5 0.7 all-gather.5.cloned.1.call-update
  7.3 0.0 all-gather.7.cloned.1.call-start
  7.3 0.7 all-gather.7.cloned.1.call-update
  8.0 0.0 all-gather.9.cloned.1.call-start
  8.1 0.7 all-gather.9.cloned.1.call-update
  8.7 0.0 reduce-scatter.4.cloned.1.call-start
  8.8 29.3 %all-gather.5.cloned.1.call-done = bf16[512,1024]{1,0:T(8,128)(2,1)} async-done(((bf16[64,1024]{1,0:T(8,128)(2,1)}), bf16[512,1024]{1,0:T(8,128)(2,1)}) %all-gather.5.cloned.1.call-update) | async-done | bytes 1048592 | tf_op jit(solution)/shard_map/all_gather | solution.py:8
  38.1 0.0 copy-start.1
  38.1 137.6 %all-gather.7.cloned.1.call-done = bf16[1024,3584]{1,0:T(8,128)(2,1)} async-done(((bf16[1024,896]{1,0:T(8,128)(2,1)}), bf16[1024,3584]{1,0:T(8,128)(2,1)}) %all-gather.7.cloned.1.call-update) | async-done | bytes 7340048 | tf_op jit(solution)/shard_map/all_gather | solution.py:13
  175.7 9.2 %convolution_convert_fusion.1 = bf16[512,3584]{1,0:T(8,128)(2,1)} fusion(bf16[512,1024]{1,0:T(8,128)(2,1)} %all-gather.5.cloned.1.call-done, bf16[1024,3584]{1,0:T(8,128)(2,1)} %all-gather.7.cloned.1.call-done), kind=kOutput, calls=%fused_computation.1 | convolution fusion | flops 3759931392 | bytes 12058624 | tf_op jit(solution)/shard_map/dot_general | solution.py:11
  184.9 0.0 reduce-scatter.4.cloned.1.call-update
  184.9 0.0 copy-start
  184.9 0.0 reduce-scatter.6.cloned.1.call-start
  185.0 128.1 %all-gather.9.cloned.1.call-done = bf16[1024,3584]{1,0:T(8,128)(2,1)} async-done(((bf16[1024,896]{1,0:T(8,128)(2,1)}), bf16[1024,3584]{1,0:T(8,128)(2,1)}) %all-gather.9.cloned.1.call-update) | async-done | bytes 7340048 | tf_op jit(solution)/shard_map/all_gather | solution.py:14
  313.1 0.0 copy-done.1
  313.1 8.5 %convolution_convert_fusion = bf16[512,3584]{1,0:T(8,128)(2,1)} fusion(bf16[512,1024]{1,0:T(8,128)(2,1)S(1)} %copy-done.1, bf16[1024,3584]{1,0:T(8,128)(2,1)} %all-gather.9.cloned.1.call-done), kind=kOutput, calls=%fused_computation | convolution fusion | flops 3759931392 | bytes 12058624 | tf_op jit(solution)/shard_map/dot_general | solution.py:11
  321.6 0.0 reduce-scatter.6.cloned.1.call-update
  321.6 0.0 copy-done
  321.6 4.0 stack.2
  325.6 5.5 all-to-all-start
  331.1 0.0 all-gather.11.cloned.1.call-start
  331.1 163.7 %reduce-scatter.4.cloned.1.call-done = bf16[64,3584]{1,0:T(8,128)(2,1)} async-done(((bf16[512,3584]{1,0:T(8,128)(2,1)}), bf16[64,3584]{1,0:T(8,128)(2,1)}) %reduce-scatter.4.cloned.1.call-update) | async-done | bytes 458768 | tf_op jit(solution)/shard_map/reduce_scatter | solution.py:16
  494.8 148.7 %reduce-scatter.6.cloned.1.call-done = bf16[64,3584]{1,0:T(8,128)(2,1)} async-done(((bf16[512,3584]{1,0:T(8,128)(2,1)}), bf16[64,3584]{1,0:T(8,128)(2,1)}) %reduce-scatter.6.cloned.1.call-update) | async-done | bytes 458768 | tf_op jit(solution)/shard_map/reduce_scatter | solution.py:19
  643.6 2.2 fusion.4
  645.8 0.0 all-gather.11.cloned.1.call-update
  645.8 0.0 reduce-scatter.8.cloned.1.call-start
  645.8 0.0 all-to-all-done
  645.8 94.3 %all-gather.11.cloned.1.call-done = bf16[512,3584]{1,0:T(8,128)(2,1)} async-done(((bf16[64,3584]{1,0:T(8,128)(2,1)}), bf16[512,3584]{1,0:T(8,128)(2,1)}) %all-gather.11.cloned.1.call-update) | async-done | bytes 3670032 | tf_op jit(solution)/shard_map/all_gather | solution.py:24
  740.1 9.2 %convolution_convert_fusion.2 = bf16[512,1024]{1,0:T(8,128)(2,1)} fusion(bf16[512,3584]{1,0:T(8,128)(2,1)} %all-gather.11.cloned.1.call-done, bf16[3584,1024]{1,0:T(8,128)(2,1)} %bitcast), kind=kOutput, calls=%fused_computation.2 | convolution fusion | flops 3758620672 | bytes 12058624 | tf_op jit(solution)/shard_map/dot_general | solution.py:38
  749.3 0.0 reduce-scatter.8.cloned.1.call-update
  749.3 30.5 %reduce-scatter.8.cloned.1.call-done = bf16[64,1024]{1,0:T(8,128)(2,1)} async-done(((bf16[512,1024]{1,0:T(8,128)(2,1)}), bf16[64,1024]{1,0:T(8,128)(2,1)}) %reduce-scatter.8.cloned.1.call-update) | async-done | bytes 131088 | tf_op jit(solution)/shard_map/reduce_scatter | solution.py:41
Async XLA Ops:
  6.5 31.6 %all-gather.5.cloned.1.call-start = ((), (), s32[]{:S(2)}) async-start(), calls=%async_computation.4 | async-start | bytes 1179648 | tf_op jit(solution)/shard_map/all_gather | solution.py:8
  7.3 168.4 %all-gather.7.cloned.1.call-start = ((), (), s32[]{:S(2)}) async-start(), calls=%async_computation.5 | async-start | bytes 9175040 | tf_op jit(solution)/shard_map/all_gather | solution.py:13
  8.0 305.1 %all-gather.9.cloned.1.call-start = ((), (), s32[]{:S(2)}) async-start(), calls=%async_computation.7 | async-start | bytes 9175040 | tf_op jit(solution)/shard_map/all_gather | solution.py:14
  8.7 486.1 %reduce-scatter.4.cloned.1.call-start = ((), (), s32[]{:S(2)}) async-start(), calls=%async_computation.6 | async-start | bytes 4128768 | tf_op jit(solution)/shard_map/reduce_scatter | solution.py:16
  38.1 275.0 %copy-start.1 = (bf16[512,1024]{1,0:T(8,128)(2,1)S(1)}, bf16[512,1024]{1,0:T(8,128)(2,1)}, u32[]{:S(2)}) copy-start(bf16[512,1024]{1,0:T(8,128)(2,1)} %all-gather.5.cloned.1.call-done) | copy-start | bytes 3145732
  184.9 136.7 %copy-start = (bf16[896,1024]{1,0:T(8,128)(2,1)S(1)}, bf16[896,1024]{1,0:T(8,128)(2,1)}, u32[]{:S(2)}) copy-start(bf16[896,1024]{1,0:T(8,128)(2,1)} %param.7) | copy-start | bytes 5505028
  184.9 458.6 %reduce-scatter.6.cloned.1.call-start = ((), (), s32[]{:S(2)}) async-start(), calls=%async_computation.8 | async-start | bytes 4128768 | tf_op jit(solution)/shard_map/reduce_scatter | solution.py:19
  325.6 320.3 %all-to-all-start = ((bf16[4,896,1024]{2,1,0:T(8,128)(2,1)}), bf16[4,896,1024]{2,1,0:T(8,128)(2,1)}, u32[]{:S(2)}, u32[]{:S(2)}) async-start(bf16[4,896,1024]{2,1,0:T(8,128)(2,1)} %stack.2), calls=%async_computation.2 | async-start | bytes 14680064 | tf_op jit(solution)/shard_map/all_to_all | solution.py:28
  331.1 409.0 %all-gather.11.cloned.1.call-start = ((), (), s32[]{:S(2)}) async-start(), calls=%async_computation.9 | async-start | bytes 4128768 | tf_op jit(solution)/shard_map/all_gather | solution.py:24
  645.8 134.0 %reduce-scatter.8.cloned.1.call-start = ((), (), s32[]{:S(2)}) async-start(), calls=%async_computation.10 | async-start | bytes 1179648 | tf_op jit(solution)/shard_map/reduce_scatter | solution.py:41
Sparse Core Ops, SparseCore 0:
  9.2 28.8 all-gather.4
  40.0 135.6 all-gather.6
  177.5 135.5 all-gather.8
  317.2 177.5 reduce-scatter.3
  499.5 143.9 reduce-scatter.5
  646.0 94.0 all-gather.10
  749.4 30.3 reduce-scatter.7
